TPU v7x, 256 devices: a whole 4x4x8 slice. The times are simulated.
256 devices in a mesh: shard: 64 (over z, y, core), help: 4 (over x).
Axes of the slice: x: 4, y: 4, z: 8, core: 2. Of those that a mesh axis runs over, the one named last changes fastest.
Arguments:
- queries: bfloat16 [65536, 768], P(('shard', 'help')), may hold values from -6 to 6
- probe_group: int32 [65536, 2], P(('shard', 'help')), may hold values from 0 to 63, all different within a row; in each aligned block of 256 rows (0 to 255, 256 to 511, ...) at most 16 rows name the same one
- probe_local: int32 [65536, 2], P(('shard', 'help')), may hold values from 0 to 3
- points: bfloat16 [262144, 768], P(('shard', 'help')), may hold values from -6 to 6
- point_cluster: int32 [64, 4096], P('shard'), may hold values from 0 to 3, never falling along the last dimension, each value on 1 to 3072 neighbouring positions
- test_matrix: bfloat16 [32, 262144], P(None, ('shard', 'help')), may hold values from -6 to 6
Outputs:
- sketch: float32 [32, 262144], P(None, ('shard', 'help'))
- regressor: float32 [256, 32, 768], P(('shard', 'help'))
Inputs may be any that keep to these rules, and one draw needn't show every extreme that they name: `probe_group`: A query's 2 groups differ. Among the 256 queries of one device (aligned blocks of rows), at most 16 pairs (q,k) name one group, and in some blocks one group is named exactly 16 times.
All inputs are finite; a program needn't handle non-finite values.
Results may differ from a plain program's by a relative error of at most 0.0037.
Values may be sent and summed in bfloat16 or wider, within the bound.
A program may use at most 64 MiB of HBM per device.

v0:
```python
import jax
import jax.numpy as jnp
from jax import lax
from jax.sharding import PartitionSpec as P

PROBES = 2
CL_DEV = 1


def masked_scores(point_rows, point_ids, query_rows, query_ids):
    feature_width = point_rows.shape[1]
    block_rows = min(512, point_rows.shape[0])
    factor = feature_width ** (-0.5)

    def score_piece(pieces):
        piece_x, piece_ids = pieces
        product = (
            lax.dot_general(
                piece_x, query_rows, (((1,), (1,)), ((), ())), preferred_element_type=jnp.float32
            )
            * factor
        )
        return jnp.where(piece_ids[:, None] == query_ids[None, :], product, 0.0).astype(
            jnp.bfloat16
        )

    stacked = lax.map(
        score_piece,
        (point_rows.reshape(-1, block_rows, feature_width), point_ids.reshape(-1, block_rows)),
    )
    return stacked.reshape(point_rows.shape[0], query_rows.shape[0])


def pack_rows(source, target, member, groups, blocks, capacity, probes):
    feature_width = source.shape[1]
    row_total = target.shape[0]
    per_block = row_total // blocks
    labels = jnp.arange(groups, dtype=jnp.int32)
    onehot_dest = (
        (target[:, None] == labels[None, :]).astype(jnp.int32).reshape(blocks, per_block, groups)
    )
    ranking = jnp.sum((jnp.cumsum(onehot_dest, axis=1) - onehot_dest) * onehot_dest, axis=2)
    position = (
        target.reshape(blocks, per_block) * (blocks * capacity)
        + jnp.arange(blocks, dtype=jnp.int32)[:, None] * capacity
        + ranking
    )
    position = position.reshape(-1)
    copied_rows = jnp.repeat(source, probes, axis=0)
    filled = (
        jnp.zeros((groups * blocks * capacity, feature_width), jnp.bfloat16)
        .at[position]
        .set(copied_rows)
    )
    labelled = jnp.full((groups * blocks * capacity,), -1, jnp.int32).at[position].set(member)
    return (
        filled.reshape(groups, blocks * capacity, feature_width),
        labelled.reshape(groups, blocks * capacity),
    )


def count_labels(ids, labels):
    return jnp.sum((ids[None, :] == labels[:, None]).astype(jnp.float32), axis=1)


def shards(queries, probe_group, probe_local, points, point_cluster, test_matrix):
    groups = lax.axis_size("shard")
    helpers = lax.axis_size("help")
    helper = lax.axis_index("help")
    feature_width = queries.shape[1]
    per_device = queries.shape[0] * PROBES
    capacity = 2 * per_device // groups
    group_clusters = CL_DEV * helpers
    own_points = points.shape[0]
    group_ids = point_cluster[0]
    own_ids = lax.dynamic_slice_in_dim(group_ids, helper * own_points, own_points, 0)
    labels = jnp.arange(group_clusters, dtype=jnp.int32)
    resident = count_labels(group_ids, labels)
    peer_rows, peer_groups, peer_local = (
        lax.all_gather(queries, "help", axis=0, tiled=True),
        lax.all_gather(probe_group, "help", axis=0, tiled=True),
        lax.all_gather(probe_local, "help", axis=0, tiled=True),
    )
    outgoing, out_ids = pack_rows(
        peer_rows,
        peer_groups.reshape(-1),
        peer_local.reshape(-1),
        groups,
        helpers,
        capacity,
        PROBES,
    )
    query_pool, pool_ids = (
        lax.all_to_all(outgoing, "shard", split_axis=0, concat_axis=0, tiled=True),
        lax.all_to_all(out_ids, "shard", split_axis=0, concat_axis=0, tiled=True),
    )
    query_rows = query_pool.reshape(-1, feature_width)
    query_ids = pool_ids.reshape(-1)
    scores = masked_scores(points, own_ids, query_rows, query_ids)
    lifted = lax.psum(
        jnp.dot(test_matrix, scores, preferred_element_type=jnp.float32), "help"
    ).astype(jnp.bfloat16)
    product = lax.dot_general(
        lifted, scores, (((1,), (1,)), ((), ())), preferred_element_type=jnp.float32
    )
    queried = count_labels(query_ids, labels)
    factor = 1.0 / jnp.sqrt((queried + 1.0) * (queried + resident))
    own_hot = (own_ids[None, :] == labels[:, None]).astype(jnp.float32)
    sketch = product * jnp.sum(factor[:, None] * own_hot, axis=0)[None, :]
    rounded = sketch.astype(jnp.bfloat16)
    hot_rows = own_hot.astype(jnp.bfloat16)
    weighted = (hot_rows[:, None, :] * rounded[None, :, :]).reshape(
        CL_DEV * lax.axis_size("help") * rounded.shape[0], own_points
    )
    summed = jnp.dot(weighted, points, preferred_element_type=jnp.float32)
    partial_sum = lax.psum_scatter(
        summed.reshape(CL_DEV * lax.axis_size("help"), rounded.shape[0], feature_width),
        "help",
        scatter_dimension=0,
        tiled=True,
    )
    scale_own = lax.dynamic_slice_in_dim(1.0 / jnp.sqrt(resident), helper * CL_DEV, CL_DEV, 0)
    regressor = partial_sum * scale_own[:, None, None]
    return (sketch, regressor)


def solution(mesh):
    in_specs = (
        P(("shard", "help"), None),
        P(("shard", "help"), None),
        P(("shard", "help"), None),
        P(("shard", "help"), None),
        P("shard", None),
        P(None, ("shard", "help")),
    )
    out_specs = (P(None, ("shard", "help")), P(("shard", "help"), None, None))
    return jax.shard_map(shards, mesh=mesh, in_specs=in_specs, out_specs=out_specs, check_vma=False)
```

profile of v0, /device:TPU:8, one launch (start us, length us, event | category | flops | bytes accessed | tf_op | source)
XLA Modules:
  0.0 307.3 jit_solution(3238835004986476215)
XLA Ops:
  7.2 0.7 all-gather.2.cloned.1.call-update
  7.9 11.3 %all_gather.9 = s32[1024,2]{0,1:T(2,128)S(1)} all-gather(s32[256,2]{0,1:T(2,128)} %param.9), channel_id=1, replica_groups=mesh['shard'=64,'help'=4] {'help'}, dimensions={0}, use_global_device_ids=true | all-gather | bytes 10240 | tf_op jit(solution)/shard_map/all_gather | solution.py:81
  19.2 0.2 copy.19
  19.4 0.3 eq.96
  19.7 0.3 eq.92
  20.1 4.8 %reduce-window.6 = s32[4,64,4,128]{3,1,2,0:T(8,128)S(1)} reduce-window(s32[4,64,4,128]{3,1,2,0:T(8,128)S(1)} %fusion.12, s32[]{:T(128)} %constant.9.clone.1), window={size=1x1x1x128 pad=0_0x0_0x0_0x127_0}, to_apply=%region_0.0 | reduce-window | flops 16646144 | bytes 1048580 | tf_op jit(solution)/shard_map/reduce-window
  24.9 0.5 slice_reduce_fusion
  25.5 0.2 fusion.11
  25.9 0.3 mul.85
  26.4 10.8 %all_gather.10 = s32[1024,2]{0,1:T(2,128)S(1)} all-gather(s32[256,2]{0,1:T(2,128)} %param.10), channel_id=1, replica_groups=mesh['shard'=64,'help'=4] {'help'}, dimensions={0}, use_global_device_ids=true | all-gather | bytes 10240 | tf_op jit(solution)/shard_map/all_gather | solution.py:82
  37.4 0.3 reshape.158
  37.7 8.1 %scatter_custom_fusion = s32[4096]{0:T(1024)S(1)} fusion(s32[2048]{0:T(1024)S(1)} %bitcast.81, s32[2048]{0:T(1024)S(1)} %reshape.158, s32[]{:T(128)} %constant.20.clone.1), kind=kCustom, calls=%fused_computation.37 | custom fusion | bytes 16388 | tf_op jit(solution)/shard_map/scatter | solution.py:55
  45.7 0.7 all_to_all.11
  46.4 12.1 %all-to-all-start = ((s32[64,1,64]{2,1,0:T(1,128)}), s32[64,1,64]{2,1,0:T(1,128)S(1)}, u32[]{:S(2)}, u32[]{:S(2)}) async-start(s32[64,1,64]{2,1,0:T(1,128)} %all_to_all.11), calls=%async_computation | async-start | bytes 65536 | tf_op jit(solution)/shard_map/all_to_all | solution.py:95
  58.6 3.0 broadcast_in_dim.20
  61.6 2.7 reshape.166
  64.3 13.9 %scatter_custom_fusion.1 = bf16[4096,768]{1,0:T(8,128)(2,1)} fusion(s32[2048]{0:T(1024)S(1)} %bitcast.82, bf16[2048,768]{1,0:T(8,128)(2,1)} %reshape.166, bf16[]{:T(256)} %constant.22.clone.1), kind=kCustom, calls=%fused_computation.10 | custom fusion | bytes 6291968 | tf_op jit(solution)/shard_map/scatter | solution.py:53
  78.2 10.6 %all-to-all-start.1 = ((bf16[64,64,768]{2,1,0:T(8,128)(2,1)}), bf16[64,64,768]{2,1,0:T(8,128)(2,1)}, u32[]{:S(2)}, u32[]{:S(2)}) async-start(bf16[64,64,768]{2,1,0:T(8,128)(2,1)} %bitcast.69), calls=%async_computation.1 | async-start | bytes 12582912 | tf_op jit(solution)/shard_map/all_to_all | solution.py:94
  88.9 0.5 broadcast.103
  89.4 0.7 fusion.19
  90.2 0.7 reduce.9
  91.3 138.7 %all-to-all-done.1 = bf16[64,64,768]{2,1,0:T(8,128)(2,1)} async-done(((bf16[64,64,768]{2,1,0:T(8,128)(2,1)}), bf16[64,64,768]{2,1,0:T(8,128)(2,1)}, u32[]{:S(2)}, u32[]{:S(2)}) %all-to-all-start.1) | async-done | bytes 6291488 | tf_op jit(solution)/shard_map/all_to_all | solution.py:94
  230.0 15.6 %while.11 = (s32[]{:T(128)}, bf16[2,512,4096]{2,1,0:T(8,128)(2,1)}, s32[2,512]{1,0:T(2,128)S(1)}, s32[64,64]{1,0:T(8,128)}, bf16[2,512,768]{2,1,0:T(8,128)(2,1)S...) while((s32[]{:T(128)}, bf16[2,512,4096]{2,1,0:T(8,128)(2,1)}, ...), condition=%wide.wide.region_6.7_spmd, body=%wide.wide.region_5.6_spmd.sunk | while | flops 3229614080 | bytes 11295833 | solution.py:27
  230.0 7.8 %fusion.35 = bf16[2,512,4096]{2,1,0:T(8,128)(2,1)} fusion(bf16[2,512,4096]{2,1,0:T(8,128)(2,1)} %get-tuple-element.131, s32[]{:T(128)} %get-tuple-element.130, bf16[4096,768]{1,0:T(8,128)(2,1)} %get-tuple-element.143, s32[4096]{0:T(1024)S(1)} %get-tuple-element.144, s32[512]{0:T(512)S(1)} %bitcast.74, ...), kind=kOutput, calls=%fused_computation.4.clone.clone.1 | convolution fusion | flops 3229614080 | bytes 11291648 | tf_op jit(solution)/shard_map/while/body/eval_jaxpr/dot_general | solution.py:18
  237.8 7.8 %fusion.35 = bf16[2,512,4096]{2,1,0:T(8,128)(2,1)} fusion(bf16[2,512,4096]{2,1,0:T(8,128)(2,1)} %get-tuple-element.131, s32[]{:T(128)} %get-tuple-element.130, bf16[4096,768]{1,0:T(8,128)(2,1)} %get-tuple-element.143, s32[4096]{0:T(1024)S(1)} %get-tuple-element.144, s32[512]{0:T(512)S(1)} %bitcast.74, ...), kind=kOutput, calls=%fused_computation.4.clone.clone.1 | convolution fusion | flops 3229614080 | bytes 11291648 | tf_op jit(solution)/shard_map/while/body/eval_jaxpr/dot_general | solution.py:18
  245.6 4.9 %convolution_bitcast_fusion = f32[32,4096]{1,0:T(8,128)S(1)} fusion(bf16[32,1024]{1,0:T(8,128)(2,1)S(1)} %copy-done, bf16[1024,4096]{1,0:T(8,128)(2,1)} %bitcast.67), kind=kOutput, calls=%fused_computation.9 | convolution fusion | flops 268435456 | bytes 8978432 | tf_op jit(solution)/shard_map/dot_general | solution.py:101
  250.5 21.6 %all-reduce.1 = bf16[32,4096]{1,0:T(8,128)(2,1)S(1)} all-reduce(f32[32,4096]{1,0:T(8,128)S(1)} %convolution_bitcast_fusion), channel_id=1, replica_groups=mesh['shard'=64,'help'=4] {'help'}, use_global_device_ids=true, to_apply=%region_7.8 | all-reduce | flops 131072 | bytes 786432 | tf_op jit(solution)/shard_map/psum | solution.py:100
  272.1 6.6 %fusion.21 = (bf16[32,1024]{1,0:T(8,128)(2,1)S(1)}, f32[32,1024]{1,0:T(8,128)}) fusion(f32[1024]{0:T(1024)S(1)} %select_reduce_fusion, bf16[32,4096]{1,0:T(8,128)(2,1)S(1)} %all-reduce.1, bf16[1024,4096]{1,0:T(8,128)(2,1)} %bitcast.68), kind=kOutput, calls=%fused_computation.46 | convolution fusion | flops 268500992 | bytes 8851456 | tf_op jit(solution)/shard_map/dot_general | solution.py:103
  278.7 1.1 fusion.7
  279.9 0.6 dynamic_slice.15
  280.5 17.8 %reduce-scatter.2.cloned.1.call-done = f32[1,32,768]{2,1,0:T(8,128)} async-done(((f32[4,32,768]{2,1,0:T(8,128)}), f32[1,32,768]{2,1,0:T(8,128)}) %reduce-scatter.2.cloned.1.call-update) | async-done | bytes 98320 | tf_op jit(solution)/shard_map/reduce_scatter | solution.py:116
  298.3 2.2 broadcast_multiply_fusion
  (34 shorter events, 1.2 us)
Async XLA Ops:
  7.2 238.4 %copy-start = (bf16[32,1024]{1,0:T(8,128)(2,1)S(1)}, bf16[32,1024]{1,0:T(8,128)(2,1)}, u32[]{:S(2)}) copy-start(bf16[32,1024]{1,0:T(8,128)(2,1)} %param.13) | copy-start | bytes 196612
  7.2 51.4 %all-gather.2.cloned.1.call-start = ((), (), s32[]{:S(2)}) async-start(), calls=%async_computation.3 | async-start | bytes 1966080 | tf_op jit(solution)/shard_map/all_gather | solution.py:80
  46.4 31.8 %all-to-all-start = ((s32[64,1,64]{2,1,0:T(1,128)}), s32[64,1,64]{2,1,0:T(1,128)S(1)}, u32[]{:S(2)}, u32[]{:S(2)}) async-start(s32[64,1,64]{2,1,0:T(1,128)} %all_to_all.11), calls=%async_computation | async-start | bytes 65536 | tf_op jit(solution)/shard_map/all_to_all | solution.py:95
  78.2 12.0 %copy-start.2 = (s32[64,1,64]{2,1,0:T(1,128)}, s32[64,1,64]{2,1,0:T(1,128)S(1)}, u32[]{:S(2)}) copy-start(s32[64,1,64]{2,1,0:T(1,128)S(1)} %all-to-all-done) | copy-start | bytes 49156
  78.2 11.2 %copy-start.3 = (s32[1,4096]{1,0:T(1,128)S(1)}, s32[1,4096]{1,0:T(1,128)}, u32[]{:S(2)}) copy-start(s32[1,4096]{1,0:T(1,128)} %param.12) | copy-start | bytes 49156
  78.2 151.7 %copy-start.1 = (bf16[1024,768]{1,0:T(8,128)(2,1)S(1)}, bf16[1024,768]{1,0:T(8,128)(2,1)}, u32[]{:S(2)}) copy-start(bf16[1024,768]{1,0:T(8,128)(2,1)} %param.11) | copy-start | bytes 4718596
  78.2 151.7 %all-to-all-start.1 = ((bf16[64,64,768]{2,1,0:T(8,128)(2,1)}), bf16[64,64,768]{2,1,0:T(8,128)(2,1)}, u32[]{:S(2)}, u32[]{:S(2)}) async-start(bf16[64,64,768]{2,1,0:T(8,128)(2,1)} %bitcast.69), calls=%async_computation.1 | async-start | bytes 12582912 | tf_op jit(solution)/shard_map/all_to_all | solution.py:94
  88.8 209.5 %reduce-scatter.2.cloned.1.call-start = ((), (), s32[]{:S(2)}) async-start(), calls=%async_computation.4 | async-start | bytes 491520 | tf_op jit(solution)/shard_map/reduce_scatter | solution.py:116
Sparse Core Ops, SparseCore 0:
  9.8 31.9 all-gather.1
  280.0 18.2 reduce-scatter.1
where the time goes:
time: 308 us; the launch traced here: 307 us
  waiting for transfers between devices  157 us (51%)
  blocking collectives  43.6 us (14%)
  local copies, waits for them, and re-layouts  32.8 us (11%)
  matrix products  28.3 us (9%)
  starting transfers between devices  22.8 us (7%)
  between operations  14.2 us (5%)
  other arithmetic  8.3 us (3%)
    all_to_all x1, waiting for transfers between devices, shards(): lax.all_to_all(outgoing, 'shard', split_axis=0, concat_axis=0, tiled=True)  139 us
    psum x1, blocking collectives, shards(): lax.psum(jnp.dot(test_matrix, scores, preferred_element_type=jnp.float32)...  21.6 us
    reduce_scatter x1, waiting for transfers between devices, shards(): lax.psum_scatter(summed.reshape(CL_DEV * lax.axis_size('help'), rounded.s...  17.8 us
    dot_general x2, matrix products, score_piece(): lax.dot_general(piece_x, query_rows, (((1,), (1,)), ((), ())), preferred_...  15.6 us
    scatter x1, local copies, waits for them, and re-layouts, pack_rows(): filled = jnp.zeros((groups * blocks * capacity, feature_width), jnp.bfloa...  13.9 us
    all_to_all x1, starting transfers between devices, shards(): lax.all_to_all(out_ids, 'shard', split_axis=0, concat_axis=0, tiled=True)  12.1 us
    all_gather x1, blocking collectives, shards(): lax.all_gather(probe_group, 'help', axis=0, tiled=True)  11.3 us
    all_gather x1, blocking collectives, shards(): lax.all_gather(probe_local, 'help', axis=0, tiled=True)  10.8 us
  transfers between devices with their start and end apart: 4, of which 2 were waited for; matrix products, arithmetic and copies ran while one was open for 12% of the time, Pallas kernels for 0%

commit v1 on v0

--- a/solution.py
+++ b/solution.py
@@ -2,9 +2,11 @@
 import jax.numpy as jnp
 from jax import lax
 from jax.sharding import PartitionSpec as P
+from jax.lax import all_gather
 
 PROBES = 2
 CL_DEV = 1
+name_roots = lambda point: jnp.sum(all_gather(point, "help"), 0)
 
 
 def masked_scores(point_rows, point_ids, query_rows, query_ids):
@@ -97,9 +99,9 @@
     query_rows = query_pool.reshape(-1, feature_width)
     query_ids = pool_ids.reshape(-1)
     scores = masked_scores(points, own_ids, query_rows, query_ids)
-    lifted = lax.psum(
-        jnp.dot(test_matrix, scores, preferred_element_type=jnp.float32), "help"
-    ).astype(jnp.bfloat16)
+    lifted = name_roots(jnp.dot(test_matrix, scores, preferred_element_type=jnp.float32)).astype(
+        jnp.bfloat16
+    )
     product = lax.dot_general(
         lifted, scores, (((1,), (1,)), ((), ())), preferred_element_type=jnp.float32
     )

time: 308 us -> 323 us (1.049)
  waiting for transfers between devices: 157 us -> 192 us
  blocking collectives: 43.6 us -> 22.1 us
    all_gather x0 -> x1, waiting for transfers between devices: none -> 28.2 us  [name_roots = lambda point: jnp.sum(all_gather(point, 'help'), 0)]
    psum x1 -> x0, blocking collectives: 21.6 us -> none  [shards(): lax.psum(jnp.dot(test_matrix, scores, preferred_element_type=jnp.float32)...]
    reduce_scatter x1, waiting for transfers between devices: 17.8 us -> 23.3 us  [shards(): lax.psum_scatter(summed.reshape(CL_DEV * lax.axis_size('help'), rounded.s...]
  transfers between devices with their start and end apart: 4 -> 5, of which waited for: 2 -> 3; matrix products, arithmetic and copies ran while one was open for 12% -> 12% of each run, Pallas kernels for 0% -> 0%
where the time goes in v1:
time: 323 us
  waiting for transfers between devices  192 us (59%)
  local copies, waits for them, and re-layouts  32.8 us (10%)
  matrix products  29.1 us (9%)
  starting transfers between devices  22.8 us (7%)
  blocking collectives  22.1 us (7%)
  between operations  14 us (4%)
  other arithmetic  10 us (3%)
    all_to_all x1, waiting for transfers between devices, shards(): lax.all_to_all(outgoing, 'shard', split_axis=0, concat_axis=0, tiled=True)  140 us
    all_gather x1, waiting for transfers between devices, name_roots = lambda point: jnp.sum(all_gather(point, 'help'), 0)  28.2 us
    reduce_scatter x1, waiting for transfers between devices, shards(): lax.psum_scatter(summed.reshape(CL_DEV * lax.axis_size('help'), rounded.s...  23.3 us
    dot_general x2, matrix products, score_piece(): lax.dot_general(piece_x, query_rows, (((1,), (1,)), ((), ())), preferred_...  15.6 us
    scatter x1, local copies, waits for them, and re-layouts, pack_rows(): filled = jnp.zeros((groups * blocks * capacity, feature_width), jnp.bfloa...  13.9 us
    all_to_all x1, starting transfers between devices, shards(): lax.all_to_all(out_ids, 'shard', split_axis=0, concat_axis=0, tiled=True)  12.1 us
    all_gather x1, blocking collectives, shards(): lax.all_gather(probe_group, 'help', axis=0, tiled=True)  11.3 us
    all_gather x1, blocking collectives, shards(): lax.all_gather(probe_local, 'help', axis=0, tiled=True)  10.8 us
  transfers between devices with their start and end apart: 5, of which 3 were waited for; matrix products, arithmetic and copies ran while one was open for 12% of the time, Pallas kernels for 0%

profile of v1, /device:TPU:8, one launch (start us, length us, event | category | flops | bytes accessed | tf_op | source)
XLA Modules:
  0.0 322.9 jit_solution(7179414293531003438)
XLA Ops:
  7.2 0.7 all-gather.4.cloned.1.call-update
  7.9 11.3 %all_gather.15 = s32[1024,2]{0,1:T(2,128)S(1)} all-gather(s32[256,2]{0,1:T(2,128)} %param.9), channel_id=1, replica_groups=mesh['shard'=64,'help'=4] {'help'}, dimensions={0}, use_global_device_ids=true | all-gather | bytes 10240 | tf_op jit(solution)/shard_map/all_gather | solution.py:83
  19.4 0.3 eq.96
  19.7 0.3 eq.92
  20.1 4.8 %reduce-window.6 = s32[4,64,4,128]{3,1,2,0:T(8,128)S(1)} reduce-window(s32[4,64,4,128]{3,1,2,0:T(8,128)S(1)} %fusion.12, s32[]{:T(128)} %constant.9.clone.1), window={size=1x1x1x128 pad=0_0x0_0x0_0x127_0}, to_apply=%region_0.0 | reduce-window | flops 16646144 | bytes 1048580 | tf_op jit(solution)/shard_map/reduce-window
  24.9 0.5 slice_reduce_fusion
  25.5 0.2 fusion.11
  25.9 0.3 mul.85
  26.4 10.8 %all_gather.16 = s32[1024,2]{0,1:T(2,128)S(1)} all-gather(s32[256,2]{0,1:T(2,128)} %param.10), channel_id=1, replica_groups=mesh['shard'=64,'help'=4] {'help'}, dimensions={0}, use_global_device_ids=true | all-gather | bytes 10240 | tf_op jit(solution)/shard_map/all_gather | solution.py:84
  37.4 0.3 reshape.158
  37.7 8.1 %scatter_custom_fusion = s32[4096]{0:T(1024)S(1)} fusion(s32[2048]{0:T(1024)S(1)} %bitcast.84, s32[2048]{0:T(1024)S(1)} %reshape.158, s32[]{:T(128)} %constant.20.clone.1), kind=kCustom, calls=%fused_computation.37 | custom fusion | bytes 16388 | tf_op jit(solution)/shard_map/scatter | solution.py:57
  45.7 0.7 all_to_all.11
  46.4 12.1 %all-to-all-start = ((s32[64,1,64]{2,1,0:T(1,128)}), s32[64,1,64]{2,1,0:T(1,128)S(1)}, u32[]{:S(2)}, u32[]{:S(2)}) async-start(s32[64,1,64]{2,1,0:T(1,128)} %all_to_all.11), calls=%async_computation | async-start | bytes 65536 | tf_op jit(solution)/shard_map/all_to_all | solution.py:97
  58.6 3.0 broadcast_in_dim.20
  61.6 2.7 reshape.166
  64.3 13.9 %scatter_custom_fusion.1 = bf16[4096,768]{1,0:T(8,128)(2,1)} fusion(s32[2048]{0:T(1024)S(1)} %bitcast.85, bf16[2048,768]{1,0:T(8,128)(2,1)} %reshape.166, bf16[]{:T(256)} %constant.22.clone.1), kind=kCustom, calls=%fused_computation.10 | custom fusion | bytes 6291968 | tf_op jit(solution)/shard_map/scatter | solution.py:55
  78.2 10.6 %all-to-all-start.1 = ((bf16[64,64,768]{2,1,0:T(8,128)(2,1)}), bf16[64,64,768]{2,1,0:T(8,128)(2,1)}, u32[]{:S(2)}, u32[]{:S(2)}) async-start(bf16[64,64,768]{2,1,0:T(8,128)(2,1)} %bitcast.70), calls=%async_computation.1 | async-start | bytes 12582912 | tf_op jit(solution)/shard_map/all_to_all | solution.py:96
  88.9 0.5 broadcast.103
  89.5 0.6 fusion.19
  90.2 139.8 %all-to-all-done.1 = bf16[64,64,768]{2,1,0:T(8,128)(2,1)} async-done(((bf16[64,64,768]{2,1,0:T(8,128)(2,1)}), bf16[64,64,768]{2,1,0:T(8,128)(2,1)}, u32[]{:S(2)}, u32[]{:S(2)}) %all-to-all-start.1) | async-done | bytes 6291488 | tf_op jit(solution)/shard_map/all_to_all | solution.py:96
  230.0 15.6 %while.11 = (s32[]{:T(128)}, bf16[2,512,4096]{2,1,0:T(8,128)(2,1)}, s32[2,512]{1,0:T(2,128)S(1)}, s32[64,64]{1,0:T(8,128)}, bf16[2,512,768]{2,1,0:T(8,128)(2,1)S...) while((s32[]{:T(128)}, bf16[2,512,4096]{2,1,0:T(8,128)(2,1)}, ...), condition=%wide.wide.region_6.7_spmd, body=%wide.wide.region_5.6_spmd.sunk | while | flops 3229614080 | bytes 11295833 | solution.py:29
  230.0 7.8 %fusion.35 = bf16[2,512,4096]{2,1,0:T(8,128)(2,1)} fusion(bf16[2,512,4096]{2,1,0:T(8,128)(2,1)} %get-tuple-element.131, s32[]{:T(128)} %get-tuple-element.130, bf16[4096,768]{1,0:T(8,128)(2,1)} %get-tuple-element.143, s32[4096]{0:T(1024)S(1)} %get-tuple-element.144, s32[512]{0:T(512)S(1)} %bitcast.77, ...), kind=kOutput, calls=%fused_computation.4.clone.clone.1 | convolution fusion | flops 3229614080 | bytes 11291648 | tf_op jit(solution)/shard_map/while/body/eval_jaxpr/dot_general | solution.py:20
  237.8 7.8 %fusion.35 = bf16[2,512,4096]{2,1,0:T(8,128)(2,1)} fusion(bf16[2,512,4096]{2,1,0:T(8,128)(2,1)} %get-tuple-element.131, s32[]{:T(128)} %get-tuple-element.130, bf16[4096,768]{1,0:T(8,128)(2,1)} %get-tuple-element.143, s32[4096]{0:T(1024)S(1)} %get-tuple-element.144, s32[512]{0:T(512)S(1)} %bitcast.77, ...), kind=kOutput, calls=%fused_computation.4.clone.clone.1 | convolution fusion | flops 3229614080 | bytes 11291648 | tf_op jit(solution)/shard_map/while/body/eval_jaxpr/dot_general | solution.py:20
  245.6 5.8 %convolution_bitcast_fusion = f32[32,4096]{1,0:T(8,128)} fusion(bf16[32,1024]{1,0:T(8,128)(2,1)S(1)} %copy-done, bf16[1024,4096]{1,0:T(8,128)(2,1)} %bitcast.68), kind=kOutput, calls=%fused_computation.9 | convolution fusion | flops 268435456 | bytes 8978432 | tf_op jit(solution)/shard_map/dot_general | solution.py:102
  251.5 0.7 reduce.9
  252.5 28.2 %all-gather.6.cloned.1.call-done = f32[128,4096]{1,0:T(8,128)} async-done(((f32[32,4096]{1,0:T(8,128)}), f32[128,4096]{1,0:T(8,128)}) %all-gather.6.cloned.1.call-update) | async-done | bytes 2097168 | tf_op jit(solution)/shard_map/all_gather | solution.py:9
  280.8 1.7 reduce_sum.49
  282.5 6.6 %fusion.21 = (bf16[32,1024]{1,0:T(8,128)(2,1)S(1)}, f32[32,1024]{1,0:T(8,128)}) fusion(f32[1024]{0:T(1024)S(1)} %select_reduce_fusion, bf16[32,4096]{1,0:T(8,128)(2,1)S(1)} %reduce_sum.49, bf16[1024,4096]{1,0:T(8,128)(2,1)} %bitcast.69), kind=kOutput, calls=%fused_computation.46 | convolution fusion | flops 268500992 | bytes 8851456 | tf_op jit(solution)/shard_map/dot_general | solution.py:105
  289.1 1.1 fusion.7
  290.3 0.6 dynamic_slice.15
  290.9 23.3 %reduce-scatter.2.cloned.1.call-done = f32[1,32,768]{2,1,0:T(8,128)} async-done(((f32[4,32,768]{2,1,0:T(8,128)}), f32[1,32,768]{2,1,0:T(8,128)}) %reduce-scatter.2.cloned.1.call-update) | async-done | bytes 98320 | tf_op jit(solution)/shard_map/reduce_scatter | solution.py:118
  314.2 2.2 broadcast_multiply_fusion
  (39 shorter events, 1.5 us)
Async XLA Ops:
  7.2 238.4 %copy-start = (bf16[32,1024]{1,0:T(8,128)(2,1)S(1)}, bf16[32,1024]{1,0:T(8,128)(2,1)}, u32[]{:S(2)}) copy-start(bf16[32,1024]{1,0:T(8,128)(2,1)} %param.13) | copy-start | bytes 196612
  7.2 51.4 %all-gather.4.cloned.1.call-start = ((), (), s32[]{:S(2)}) async-start(), calls=%async_computation.3 | async-start | bytes 1966080 | tf_op jit(solution)/shard_map/all_gather | solution.py:82
  46.4 31.8 %all-to-all-start = ((s32[64,1,64]{2,1,0:T(1,128)}), s32[64,1,64]{2,1,0:T(1,128)S(1)}, u32[]{:S(2)}, u32[]{:S(2)}) async-start(s32[64,1,64]{2,1,0:T(1,128)} %all_to_all.11), calls=%async_computation | async-start | bytes 65536 | tf_op jit(solution)/shard_map/all_to_all | solution.py:97
  78.2 11.9 %copy-start.2 = (s32[64,1,64]{2,1,0:T(1,128)}, s32[64,1,64]{2,1,0:T(1,128)S(1)}, u32[]{:S(2)}) copy-start(s32[64,1,64]{2,1,0:T(1,128)S(1)} %all-to-all-done) | copy-start | bytes 49156
  78.2 11.2 %copy-start.4 = (s32[1,4096]{1,0:T(1,128)S(1)}, s32[1,4096]{1,0:T(1,128)}, u32[]{:S(2)}) copy-start(s32[1,4096]{1,0:T(1,128)} %param.12) | copy-start | bytes 49156
  78.2 151.7 %copy-start.1 = (bf16[1024,768]{1,0:T(8,128)(2,1)S(1)}, bf16[1024,768]{1,0:T(8,128)(2,1)}, u32[]{:S(2)}) copy-start(bf16[1024,768]{1,0:T(8,128)(2,1)} %param.11) | copy-start | bytes 4718596
  78.2 151.7 %all-to-all-start.1 = ((bf16[64,64,768]{2,1,0:T(8,128)(2,1)}), bf16[64,64,768]{2,1,0:T(8,128)(2,1)}, u32[]{:S(2)}, u32[]{:S(2)}) async-start(bf16[64,64,768]{2,1,0:T(8,128)(2,1)} %bitcast.70), calls=%async_computation.1 | async-start | bytes 12582912 | tf_op jit(solution)/shard_map/all_to_all | solution.py:96
  88.8 191.9 %all-gather.6.cloned.1.call-start = ((), (), s32[]{:S(2)}) async-start(), calls=%async_computation.5 | async-start | bytes 2621440 | tf_op jit(solution)/shard_map/all_gather | solution.py:9
  245.6 5.9 %copy-start.3 = (s32[64,64]{1,0:T(8,128)S(1)}, s32[64,64]{1,0:T(8,128)}, u32[]{:S(2)}) copy-start(s32[64,64]{1,0:T(8,128)} %get-tuple-element.161) | copy-start | bytes 49156
  251.4 62.8 %reduce-scatter.2.cloned.1.call-start = ((), (), s32[]{:S(2)}) async-start(), calls=%async_computation.4 | async-start | bytes 491520 | tf_op jit(solution)/shard_map/reduce_scatter | solution.py:118
Sparse Core Ops, SparseCore 0:
  9.8 31.9 all-gather.3
  251.5 29.2 all-gather.5
  290.4 23.7 reduce-scatter.1
